TPU v7x, 32 devices: a whole 2x2x4 slice. The times are simulated.
32 devices in a mesh: pen: 16 (over z, x, core), coil: 2 (over y).
Axes of the slice: x: 2, y: 2, z: 4, core: 2. Of those that a mesh axis runs over, the one named last changes fastest.
Arguments:
- image_field: float32 [512, 512, 2, 128], P('pen'), may hold values from -6 to 6
- coil_maps: bfloat16 [2, 512, 512, 2, 128], P('coil', 'pen'), may hold values from -5 to 5
- samples: bfloat16 [2, 4096, 128, 2, 128], P('coil', 'pen'), may hold values from -6 to 6
- kernels: bfloat16 [4096, 128, 128], P('pen'), may hold values from -0.5 to 0.5
- tile_of_block: int32 [4096], P('pen'), may hold values from 0 to 2047, as said below
Outputs:
- gradient: float32 [512, 512, 2, 128], P('pen', 'coil')
Inputs may be any that keep to these rules, and one draw needn't show every extreme that they name: The tile of every block lies with the block: tile_of_block[b] // 128 == b // 256; every tile is named by at least one block.
All inputs are finite; a program needn't handle non-finite values.
Results may differ from a plain program's by a relative error of at most 0.012.
Values may be sent and summed in bfloat16 or wider, within the bound.
No kernel may reach another device: no remote copies, remote signals or barrier semaphores. Data moves between devices by JAX's collectives and lax.ppermute only.
A program may use at most 256 MiB of HBM per device.

v0:
```python
import math
import jax
import jax.numpy as jnp
from jax import lax
from jax.sharding import PartitionSpec as P

NL = 512
NZ = 128
TILE = 128
tv_weight = 2.0


def shifted(shard, axis, by):
    length = lax.axis_size(axis)
    pairs = [(i, i + by) for i in range(length) if 0 <= i + by < length]
    return lax.ppermute(shard, axis, pairs)


def dft_tables(length, direction):
    index = lax.iota(jnp.int32, length)
    phase = index[:, None] * index[None, :] % length
    angle = 2.0 * math.pi / length * phase.astype(jnp.float32)
    cosine = jnp.cos(angle) / math.sqrt(length)
    sine = direction * jnp.sin(angle) / math.sqrt(length)
    table = jnp.stack([jnp.stack([cosine, sine], -1), jnp.stack([-sine, cosine], -1)], 1)
    high_part = table.astype(jnp.bfloat16)
    low_part = (table - high_part.astype(jnp.float32)).astype(jnp.bfloat16)
    return (high_part, low_part)


def along_second(tables, values):
    first = jnp.einsum("kpxr,yxrz->ykpz", tables[0], values, preferred_element_type=jnp.float32)
    return first + jnp.einsum(
        "kpxr,yxrz->ykpz", tables[1], values, preferred_element_type=jnp.float32
    )


def along_first(tables, values):
    first = jnp.einsum("kpyr,yxrz->kxpz", tables[0], values, preferred_element_type=jnp.float32)
    return first + jnp.einsum(
        "kpyr,yxrz->kxpz", tables[1], values, preferred_element_type=jnp.float32
    )


def flux_fields(extended, first_row, first_col):
    center = extended[:-1, :-1]
    row_ids = first_row + jnp.arange(center.shape[0])
    col_ids = first_col + jnp.arange(center.shape[1])
    diff_y = (extended[1:, :-1] - center) * (row_ids != NL - 1)[:, None, None, None]
    diff_x = (extended[:-1, 1:] - center) * (col_ids != NL - 1)[None, :, None, None]
    diff_z = jnp.concatenate(
        [center[..., 1:] - center[..., :-1], jnp.zeros_like(center[..., :1])], 3
    )
    norm_den = jnp.sqrt(
        1.0 + jnp.sum(diff_y * diff_y + diff_x * diff_x + diff_z * diff_z, axis=2, keepdims=True)
    )
    inside = ((row_ids >= 0)[:, None] & (col_ids >= 0)[None, :]).astype(jnp.float32)[
        :, :, None, None
    ]
    return (diff_y / norm_den * inside, diff_x / norm_den * inside, diff_z / norm_den * inside)


def plane_divergence(flux_z):
    return jnp.concatenate([jnp.zeros_like(flux_z[..., :1]), flux_z[..., :-1]], 3) - flux_z


def on_device(image_field, coil_maps, samples, kernels, tile_of_block):
    own_rows = image_field.shape[0]
    pen_count = lax.axis_size("pen")
    half_cols = NL // lax.axis_size("coil")
    local_cols = NL // pen_count
    pen_id = lax.axis_index("pen")
    coil_id = lax.axis_index("coil")
    row_start = pen_id * own_rows
    col_start = coil_id * half_cols
    map_real = coil_maps[0, :, :, 0].astype(jnp.float32)
    map_imag = coil_maps[0, :, :, 1].astype(jnp.float32)
    field_real = image_field[:, :, 0]
    field_imag = image_field[:, :, 1]
    coil_image = jnp.stack(
        [
            map_real * field_real - map_imag * field_imag,
            map_real * field_imag + map_imag * field_real,
        ],
        2,
    ).astype(jnp.bfloat16)
    forward_tab = dft_tables(NL, 1.0)
    adjoint_tab = dft_tables(NL, -1.0)
    rows_spectrum = along_second(forward_tab, coil_image).astype(jnp.bfloat16)
    kspace_grid = along_first(
        forward_tab, lax.all_to_all(rows_spectrum, "pen", split_axis=1, concat_axis=0, tiled=True)
    ).astype(jnp.bfloat16)
    grid_tiles = (
        kspace_grid.reshape(NL // TILE, TILE, local_cols, 2 * NZ)
        .transpose(2, 0, 1, 3)
        .reshape(-1, TILE, 2 * NZ)
    )
    tile_count = grid_tiles.shape[0]
    local_ids = tile_of_block - pen_id * tile_count
    picked = jnp.take(grid_tiles, local_ids, axis=0)
    predicted = jnp.einsum("bst,btc->bsc", kernels, picked, preferred_element_type=jnp.float32)
    measured = samples[0].reshape(predicted.shape).astype(jnp.float32)
    misfit = (predicted - measured).astype(jnp.bfloat16)
    back_terms = jnp.einsum("bst,bsc->btc", kernels, misfit, preferred_element_type=jnp.float32)
    onehot = (local_ids[:, None] == jnp.arange(tile_count, dtype=jnp.int32)[None, :]).astype(
        jnp.float32
    )
    back_tiles = jnp.einsum(
        "bl,btc->ltc", onehot, back_terms, precision=lax.Precision.HIGHEST
    ).astype(jnp.bfloat16)
    back_grid = (
        back_tiles.reshape(local_cols, NL // TILE, TILE, 2 * NZ)
        .transpose(1, 2, 0, 3)
        .reshape(NL, local_cols, 2, NZ)
    )
    back_rows = along_first(adjoint_tab, back_grid).astype(jnp.bfloat16)
    back_image = along_second(
        adjoint_tab, lax.all_to_all(back_rows, "pen", split_axis=0, concat_axis=1, tiled=True)
    )
    back_real = back_image[:, :, 0]
    back_imag = back_image[:, :, 1]
    coil_term = jnp.stack(
        [map_real * back_real + map_imag * back_imag, map_real * back_imag - map_imag * back_real],
        2,
    )
    summed = lax.psum(coil_term, "coil")
    data_gradient = lax.dynamic_slice_in_dim(summed, col_start, half_cols, 1)
    padded = jnp.pad(image_field, ((0, 0), (1, 1), (0, 0), (0, 0)))
    window = lax.dynamic_slice_in_dim(padded, col_start, half_cols + 2, 1)
    upper_row = shifted(window[:1], "pen", -1)
    extended = jnp.concatenate([window, upper_row], 0)
    flux_y, flux_x, flux_z = flux_fields(extended, row_start, col_start - 1)
    lower_row = shifted(flux_y[-1:], "pen", 1)
    flux_before = jnp.concatenate([lower_row, flux_y[:-1]], 0)
    tv_part = (
        flux_before[:, 1:]
        - flux_y[:, 1:]
        + flux_x[:, :-1]
        - flux_x[:, 1:]
        + plane_divergence(flux_z[:, 1:])
    )
    return data_gradient + tv_weight * tv_part


def solution(mesh):
    in_specs = (
        P("pen", None, None, None),
        P("coil", "pen", None, None, None),
        P("coil", "pen", None, None, None),
        P("pen", None, None),
        P("pen"),
    )
    out_specs = P("pen", "coil", None, None)
    return jax.shard_map(
        on_device, mesh=mesh, in_specs=in_specs, out_specs=out_specs, check_vma=False
    )
```

profile of v0, /device:TPU:0, one launch (start us, length us, event | category | flops | bytes accessed | tf_op | source)
XLA Modules:
  0.0 1350.3 jit_solution(1019381093489078857)
XLA Ops:
  20.2 25.0 %copy.32 = f32[32,512,2,128]{1,3,2,0:T(8,128)} copy(f32[32,512,2,128]{3,2,1,0:T(2,128)} %param.5) | data formatting | bytes 33554432 | tf_op args[0]
  45.2 17.5 %fusion.90 = (bf16[1,32,512,1,128]{4,3,2,1,0:T(2,128)(2,1)}, bf16[1,32,512,1,128]{4,3,2,1,0:T(2,128)(2,1)}) fusion(bf16[1,32,512,2,128]{4,3,2,1,0:T(2,128)(2,1)} %param.6), kind=kLoop, calls=%fused_computation.127 | loop fusion | bytes 16777216 | tf_op jit(solution)/shard_map/slice | solution.py:76
  62.7 18.3 %copy.75 = bf16[1,32,512,1,128]{2,4,1,3,0:T(8,128)(2,1)} copy(bf16[1,32,512,1,128]{4,3,2,1,0:T(2,128)(2,1)} %get-tuple-element.13) | data formatting | bytes 8388608
  81.0 18.3 %copy.76 = bf16[1,32,512,1,128]{2,4,1,3,0:T(8,128)(2,1)} copy(bf16[1,32,512,1,128]{4,3,2,1,0:T(2,128)(2,1)} %get-tuple-element.14) | data formatting | bytes 8388608
  126.7 17.4 %fusion.37 = bf16[32,512,2,128]{1,3,2,0:T(8,128)(2,1)} fusion(bf16[32,512,1,128]{1,3,2,0:T(8,128)(2,1)} %copy-done.4, bf16[32,512,1,128]{1,3,2,0:T(8,128)(2,1)} %copy-done.3, f32[32,128,512,2,1]{2,1,4,3,0:T(8,128)} %fusion.36, f32[512,1,512,2]{2,0,3,1:T(8,128)} %copy-done.8, f32[512,1,512,2]{2,0,3,1:T(8,128)} %copy-done.10), kind=kOutput, calls=%fused_computation.63 | convolution fusion | flops 8620343296 | bytes 37748736 | tf_op jit(solution)/shard_map/kpxr,yxrz->ykpz/dot_general | solution.py:33
  144.1 21.3 %copy.35 = bf16[32,512,2,128]{3,2,0,1:T(2,128)(2,1)} copy(bf16[32,512,2,128]{1,3,2,0:T(8,128)(2,1)} %fusion.37) | data formatting | bytes 16777216 | tf_op jit(solution)/shard_map/convert_element_type | solution.py:89
  172.9 45.1 %copy.42 = f32[1,256,128,2,128]{2,4,3,1,0:T(8,128)} copy(bf16[1,256,128,2,128]{4,3,2,1,0:T(2,128)(2,1)} %param.7) | data formatting | bytes 50331648 | tf_op jit(solution)/shard_map/convert_element_type | solution.py:102
  218.0 105.4 %all-to-all-done = bf16[32,512,2,128]{3,2,0,1:T(2,128)(2,1)} async-done(((bf16[32,512,2,128]{3,2,0,1:T(2,128)(2,1)}), bf16[32,512,2,128]{3,2,0,1:T(2,128)(2,1)}, u32[]{:S(2)}, u32[]{:S(2)}) %all-to-all-start) | async-done | bytes 8388640 | tf_op jit(solution)/shard_map/all_to_all | solution.py:91
  323.4 16.5 %copy.36 = bf16[32,512,2,128]{3,1,2,0:T(8,128)(2,1)} copy(bf16[32,512,2,128]{3,2,0,1:T(2,128)(2,1)} %all-to-all-done) | data formatting | bytes 16777216 | tf_op jit(solution)/shard_map/all_to_all | solution.py:91
  379.7 17.1 %fusion.38 = bf16[512,32,2,128]{0,3,2,1:T(8,128)(2,1)} fusion(bf16[512,32,2,128,1]{0,3,2,4,1:T(8,128)(2,1)} %copy.55, f32[32,128,512,2,1]{2,1,4,3,0:T(8,128)} %fusion.68, f32[512,1,512,2]{2,0,3,1:T(8,128)S(1)} %copy-done.9, f32[512,1,512,2]{2,0,3,1:T(8,128)S(1)} %copy-done.11), kind=kOutput, calls=%fused_computation.64 | convolution fusion | flops 8603566080 | bytes 37748736 | tf_op jit(solution)/shard_map/kpyr,yxrz->kxpz/dot_general | solution.py:40
  435.7 38.4 %fusion.10 = f32[256,128,256]{1,2,0:T(8,128)} fusion(bf16[256,128,128]{2,1,0:T(8,128)(2,1)} %param.8, f32[256,128,256]{1,2,0:T(8,128)} %bitcast.151, bf16[256,128,256]{2,1,0:T(8,128)(2,1)} %gather_fusion, pred[256]{0:T(512)(128)(4,1)S(1)} %get-tuple-element.5), kind=kOutput, calls=%fused_computation.30 | convolution fusion | flops 4320133120 | bytes 92274944 | tf_op jit(solution)/shard_map/bst,bsc->btc/dot_general | solution.py:104
  474.1 33.4 %copy.43 = f32[256,128,256]{2,0,1:T(8,128)} copy(f32[256,128,256]{1,2,0:T(8,128)} %fusion.10) | data formatting | bytes 67108864 | tf_op jit(solution)/shard_map/bst,bsc->btc/dot_general | solution.py:104
  507.5 20.8 %convolution_convert_fusion = bf16[128,128,256]{2,0,1:T(8,128)(2,1)} fusion(f32[256,128,256]{2,0,1:T(8,128)} %copy.43, s32[256]{0:T(256)S(1)} %get-tuple-element.6), kind=kOutput, calls=%fused_computation.60 | convolution fusion | flops 12889128960 | bytes 41944064 | tf_op jit(solution)/shard_map/bl,btc->ltc/dot_general | solution.py:108
  540.8 18.0 %copy.44 = bf16[4,128,32,256]{1,0,3,2:T(4,128)(2,1)} copy(bf16[4,128,32,256]{3,0,2,1:T(4,128)(2,1)} %bitcast.155) | data formatting | bytes 16777216 | tf_op jit(solution)/shard_map/transpose | solution.py:113
  572.1 16.8 %fusion.32 = f32[32,128,512,2,1]{2,1,4,3,0:T(8,128)} fusion(bf16[512,32,2,128,1]{0,3,2,1,4:T(8,128)(2,1)} %reshape.238, f32[512,1,512,2]{2,0,3,1:T(8,128)} %get-tuple-element.17, f32[512,1,512,2]{2,0,3,1:T(8,128)S(1)} %copy-done.5), kind=kOutput, calls=%fused_computation.57 | convolution fusion | flops 8594128896 | bytes 29360128 | tf_op jit(solution)/shard_map/kpyr,yxrz->kxpz/dot_general | solution.py:39
  588.9 16.9 %fusion.39 = bf16[512,32,2,128]{0,3,2,1:T(8,128)(2,1)} fusion(bf16[512,32,2,128,1]{0,3,2,1,4:T(8,128)(2,1)} %reshape.238, f32[32,128,512,2,1]{2,1,4,3,0:T(8,128)} %fusion.32, f32[512,1,512,2]{2,0,3,1:T(8,128)S(1)} %copy-done.6, f32[512,1,512,2]{2,0,3,1:T(8,128)S(1)} %copy-done.5), kind=kOutput, calls=%fused_computation.65 | convolution fusion | flops 8603566080 | bytes 37748736 | tf_op jit(solution)/shard_map/kpyr,yxrz->kxpz/dot_general | solution.py:40
  605.8 21.2 %copy.45 = bf16[512,32,2,128]{3,2,1,0:T(2,128)(2,1)} copy(bf16[512,32,2,128]{0,3,2,1:T(8,128)(2,1)} %fusion.39) | data formatting | bytes 16777216 | tf_op jit(solution)/shard_map/convert_element_type | solution.py:116
  627.0 218.8 %all_to_all.36 = bf16[512,32,2,128]{3,2,1,0:T(2,128)(2,1)} all-to-all(bf16[512,32,2,128]{3,2,1,0:T(2,128)(2,1)} %copy.45), channel_id=1, replica_groups=mesh['pen'=16,'coil'=2] {'pen'}, dimensions={0} | all-to-all | bytes 16777216 | tf_op jit(solution)/shard_map/all_to_all | solution.py:118
  878.6 19.0 %fusion.3 = f32[32,512,2,128]{1,3,2,0:T(8,128)} fusion(f32[32,128,512,2,1]{2,1,4,3,0:T(8,128)} %fusion.65, bf16[32,512,2,128,1]{3,1,2,4,0:T(8,128)(2,1)} %bitcast.158, f32[512,1,512,2]{2,0,3,1:T(8,128)} %get-tuple-element.17, f32[512,1,512,2]{2,0,3,1:T(8,128)S(1)} %copy-done.5), kind=kOutput, calls=%fused_computation.12 | convolution fusion | flops 8599371776 | bytes 46137344 | tf_op jit(solution)/shard_map/kpxr,yxrz->ykpz/dot_general | solution.py:33
  937.5 21.1 %fusion.15 = f32[32,257,2,127]{1,3,2,0:T(8,128)} fusion(s32[]{:T(128)S(6)} %select_n.65, s32[]{:T(128)S(6)} %add.172, f32[32,512,2,128]{1,3,2,0:T(8,128)} %copy.32), kind=kLoop, calls=%fused_computation.33 | loop fusion | flops 2088896 | bytes 25132808 | tf_op jit(solution)/shard_map/sub | solution.py:52
  958.7 23.7 %add_reduce_fusion = f32[32,257,128]{1,2,0:T(8,128)} fusion(f32[32,257,2,127]{1,3,2,0:T(8,128)} %fusion.15, f32[257]{0:T(512)S(1)} %get-tuple-element.21, s32[]{:T(128)S(6)} %select_n.65, f32[32,512,2,128]{1,3,2,0:T(8,128)} %copy.32, s32[]{:T(128)S(6)} %add.171, f32[32]{0:T(128)S(1)} %get-tuple-element.22, f32[1,258,2,128]{1,3,2,0:T(8,128)S(1)} %collective-permute-done, ...), kind=kLoop, calls=%fused_computation.40 | loop fusion | flops 22106112 | bytes 38062988 | tf_op jit(solution)/shard_map/reduce_sum | solution.py:55
  986.8 39.5 %divide_multiply_fusion.2 = (f32[32,257,2,128]{1,3,2,0:T(8,128)}, f32[32,257,2,128]{1,3,2,0:T(8,128)}, f32[32,257,2,128]{1,3,2,0:T(8,128)}) fusion(f32[32,257]{1,0:T(8,128)S(1)} %and_convert_fusion, f32[32,257,128]{1,2,0:T(8,128)S(1)} %add_sqrt_fusion, f32[32]{0:T(128)S(1)} %get-tuple-element.22, s32[]{:T(128)S(6)} %select_n.65, ...), kind=kLoop, calls=%fused_computation.39 | loop fusion | flops 23158784 | bytes 63360012 | tf_op jit(solution)/shard_map/mul | solution.py:60
  1050.2 250.9 %all-reduce.5.cloned.1.call-done = f32[32,512,2,128]{1,3,2,0:T(8,128)} async-done(((f32[32,512,2,128]{1,3,2,0:T(8,128)}), f32[32,512,2,128]{1,3,2,0:T(8,128)}) %all-reduce.5.cloned.1.call-update) | async-done | bytes 16777232 | tf_op jit(solution)/shard_map/psum | solution.py:126
  1301.1 28.7 %fusion.30 = f32[32,256,2,128]{1,3,2,0:T(8,128)} fusion(f32[32,257,2,128]{1,3,2,0:T(8,128)} %get-tuple-element.15, f32[32,257,2,128]{1,3,2,0:T(8,128)} %get-tuple-element.12, f32[32,257,2,128]{1,3,2,0:T(8,128)} %get-tuple-element.11, f32[31,257,2,128]{1,3,2,0:T(8,128)} %slice.90, f32[1,257,2,128]{1,3,2,0:T(8,128)S(1)} %collective-permute-done.1, ...), kind=kLoop, calls=%fused_computation.50 | loop fusion | flops 16777216 | bytes 67076100 | tf_op jit(solution)/shard_map/add | solution.py:142
  (65 shorter events, 267.2 us)
Async XLA Ops:
  99.3 10.2 copy-start.1
  99.3 10.2 copy-start.2
  109.4 3.3 copy-start.3
  109.4 4.4 copy-start.4
  112.6 1.9 copy-start.8
  112.6 2.6 copy-start.10
  165.4 158.0 %all-to-all-start = ((bf16[32,512,2,128]{3,2,0,1:T(2,128)(2,1)}), bf16[32,512,2,128]{3,2,0,1:T(2,128)(2,1)}, u32[]{:S(2)}, u32[]{:S(2)}) async-start(bf16[32,512,2,128]{3,2,0,1:T(2,128)(2,1)} %copy.35), calls=%async_computation | async-start | bytes 16777216 | tf_op jit(solution)/shard_map/all_to_all | solution.py:91
  172.9 1128.3 %all-reduce.5.cloned.1.call-start = ((), (), s32[]{:S(2)}) async-start(), calls=%async_computation.2 | async-start | bytes 33554432 | tf_op jit(solution)/shard_map/psum | solution.py:126
  172.9 45.1 %copy-start.12 = (s32[256]{0:T(256)S(1)}, s32[256]{0:T(256)}, u32[]{:S(2)}) copy-start(s32[256]{0:T(256)} %param.9) | copy-start | bytes 3076
  349.2 14.0 %copy-start.9 = (f32[512,1,512,2]{2,0,3,1:T(8,128)S(1)}, f32[512,1,512,2]{2,0,3,1:T(8,128)}, u32[]{:S(2)}) copy-start(f32[512,1,512,2]{2,0,3,1:T(8,128)} %copy-done.8) | copy-start | bytes 6291460
  363.2 16.4 %copy-start.11 = (f32[512,1,512,2]{2,0,3,1:T(8,128)S(1)}, f32[512,1,512,2]{2,0,3,1:T(8,128)}, u32[]{:S(2)}) copy-start(f32[512,1,512,2]{2,0,3,1:T(8,128)} %copy-done.10) | copy-start | bytes 6291460
  558.8 13.2 copy-start.5
  572.1 16.8 %copy-start.6 = (f32[512,1,512,2]{2,0,3,1:T(8,128)S(1)}, f32[512,1,512,2]{2,0,3,1:T(8,128)}, u32[]{:S(2)}) copy-start(f32[512,1,512,2]{2,0,3,1:T(8,128)} %get-tuple-element.17) | copy-start | bytes 6291460
  854.7 9.1 copy-start.7
  878.6 19.0 %copy-start = (bf16[1,32,512,1,128]{2,4,1,3,0:T(8,128)(2,1)S(1)}, bf16[1,32,512,1,128]{2,4,1,3,0:T(8,128)(2,1)}, u32[]{:S(2)}) copy-start(bf16[1,32,512,1,128]{2,4,1,3,0:T(8,128)(2,1)} %copy.75) | copy-start | bytes 12582916
  923.1 35.6 %collective-permute-start = (f32[1,258,2,128]{1,3,2,0:T(8,128)S(1)}, f32[1,258,2,128]{1,3,2,0:T(8,128)S(1)}, u32[]{:S(2)}, u32[]{:S(2)}) collective-permute-start(f32[1,258,2,128]{1,3,2,0:T(8,128)S(1)} %pad_dynamic-slice_fusion.4), channel_id=1, source_target_pairs={{2,0},{4,2},{6,4},{8,6},{10,8},{12,10},{14,12},{16,14},{18,16},{20... | collective-permute-start | bytes 792584 | tf_op jit(solution)/shard_map/ppermute | solution.py:16
  1027.3 23.0 %collective-permute-start.1 = (f32[1,257,2,128]{1,3,2,0:T(8,128)S(1)}, f32[1,257,2,128]{1,3,2,0:T(8,128)S(1)}, u32[]{:S(2)}, u32[]{:S(2)}) collective-permute-start(f32[1,257,2,128]{1,3,2,0:T(8,128)S(1)} %slice.89), channel_id=1, source_target_pairs={{0,2},{2,4},{4,6},{6,8},{8,10},{10,12},{12,14},{14,16},{16,18},{18... | collective-permute-start | bytes 789512 | tf_op jit(solution)/shard_map/ppermute | solution.py:16
Sparse Core Ops, SparseCore 0:
  922.0 379.0 all-reduce.4
where the time goes:
time: 1360 us; the launch traced here: 1350 us
  local copies, waits for them, and re-layouts  393 us (29%)
  waiting for transfers between devices  356 us (26%)
  blocking collectives  219 us (16%)
  matrix products  189 us (14%)
  other arithmetic  169 us (12%)
  between operations  14.1 us (1%)
    psum x1, waiting for transfers between devices, on_device(): summed = lax.psum(coil_term, 'coil')  251 us
    all_to_all x1, blocking collectives, on_device(): lax.all_to_all(back_rows, 'pen', split_axis=0, concat_axis=1, tiled=True)  219 us
    all_to_all x1, waiting for transfers between devices, on_device(): lax.all_to_all(rows_spectrum, 'pen', split_axis=1, concat_axis=0, tiled=T...  105 us
    unnamed x29, local copies, waits for them, and re-layouts  64.2 us
    convert_element_type x1, local copies, waits for them, and re-layouts, on_device(): measured = samples[0].reshape(predicted.shape).astype(jnp.float32)  45.1 us
    all_to_all x3, local copies, waits for them, and re-layouts, on_device(): lax.all_to_all(rows_spectrum, 'pen', split_axis=1, concat_axis=0, tiled=T...  39.8 us
    mul x1, other arithmetic, flux_fields(): diff_y / norm_den * inside  39.5 us
    dot_general x1, matrix products, on_device(): jnp.einsum('bst,bsc->btc', kernels, misfit, preferred_element_type=jnp.fl...  38.4 us
  transfers between devices with their start and end apart: 4, of which 2 were waited for; matrix products, arithmetic and copies ran while one was open for 13% of the time, Pallas kernels for 0%

commit v1 on v0

--- a/solution.py
+++ b/solution.py
@@ -123,7 +123,8 @@
         [map_real * back_real + map_imag * back_imag, map_real * back_imag - map_imag * back_real],
         2,
     )
-    summed = lax.psum(coil_term, "coil")
+    handle_notes = lambda local_x: jax.lax.all_gather(local_x, "coil").sum(axis=0)
+    summed = handle_notes(coil_term)
     data_gradient = lax.dynamic_slice_in_dim(summed, col_start, half_cols, 1)
     padded = jnp.pad(image_field, ((0, 0), (1, 1), (0, 0), (0, 0)))
     window = lax.dynamic_slice_in_dim(padded, col_start, half_cols + 2, 1)

time: 1360 us -> 1430 us (1.051)
  local copies, waits for them, and re-layouts: 393 us -> 428 us
  other arithmetic: 169 us -> 189 us
    all_gather x0 -> x1, waiting for transfers between devices: none -> 257 us  [on_device(): jax.lax.all_gather(local_x, 'coil').sum(axis=0)]
    psum x1 -> x0, waiting for transfers between devices: 251 us -> none  [on_device(): summed = lax.psum(coil_term, 'coil')]
    reduce_sum x0 -> x1, other arithmetic: none -> 19.1 us  [on_device(): jax.lax.all_gather(local_x, 'coil').sum(axis=0)]
    another operation x0 -> x1, local copies, waits for them, and re-layouts: none -> 17.4 us  [on_device(): jnp.stack([map_real * back_real + map_imag * back_imag, map_real * back_i...]
    unnamed x29 -> x30, local copies, waits for them, and re-layouts: 64.2 us -> 73.2 us
  transfers between devices with their start and end apart: 4 -> 4, of which waited for: 2 -> 2; matrix products, arithmetic and copies ran while one was open for 13% -> 15% of each run, Pallas kernels for 0% -> 0%
where the time goes in v1:
time: 1430 us; the launch traced here: 1410 us
  local copies, waits for them, and re-layouts  428 us (30%)
  waiting for transfers between devices  363 us (25%)
  blocking collectives  219 us (15%)
  other arithmetic  189 us (13%)
  matrix products  189 us (13%)
    all_gather x1, waiting for transfers between devices, on_device(): jax.lax.all_gather(local_x, 'coil').sum(axis=0)  257 us
    all_to_all x1, blocking collectives, on_device(): lax.all_to_all(back_rows, 'pen', split_axis=0, concat_axis=1, tiled=True)  219 us
    all_to_all x1, waiting for transfers between devices, on_device(): lax.all_to_all(rows_spectrum, 'pen', split_axis=1, concat_axis=0, tiled=T...  105 us
    unnamed x30, local copies, waits for them, and re-layouts  73.2 us
    convert_element_type x1, local copies, waits for them, and re-layouts, on_device(): measured = samples[0].reshape(predicted.shape).astype(jnp.float32)  45.1 us
    all_to_all x3, local copies, waits for them, and re-layouts, on_device(): lax.all_to_all(rows_spectrum, 'pen', split_axis=1, concat_axis=0, tiled=T...  39.8 us
    dot_general x1, matrix products, on_device(): jnp.einsum('bst,bsc->btc', kernels, misfit, preferred_element_type=jnp.fl...  38.3 us
    mul x1, other arithmetic, flux_fields(): diff_y / norm_den * inside  36.8 us
  transfers between devices with their start and end apart: 4, of which 2 were waited for; matrix products, arithmetic and copies ran while one was open for 15% of the time, Pallas kernels for 0%

profile of v1, /device:TPU:0, one launch (start us, length us, event | category | flops | bytes accessed | tf_op | source)
XLA Modules:
  0.0 1414.1 jit_solution(6243430475982261849)
XLA Ops:
  20.2 25.0 %copy.28 = f32[32,512,2,128]{1,3,2,0:T(8,128)} copy(f32[32,512,2,128]{3,2,1,0:T(2,128)} %param.5) | data formatting | bytes 33554432 | tf_op args[0]
  45.2 17.7 %fusion.90 = (bf16[1,32,512,1,128]{4,3,2,1,0:T(2,128)(2,1)}, bf16[1,32,512,1,128]{4,3,2,1,0:T(2,128)(2,1)}) fusion(bf16[1,32,512,2,128]{4,3,2,1,0:T(2,128)(2,1)} %param.6), kind=kLoop, calls=%fused_computation.128 | loop fusion | bytes 16777216 | tf_op jit(solution)/shard_map/slice | solution.py:76
  62.9 18.3 %copy.74 = bf16[1,32,512,1,128]{2,4,1,3,0:T(8,128)(2,1)} copy(bf16[1,32,512,1,128]{4,3,2,1,0:T(2,128)(2,1)} %get-tuple-element.13) | data formatting | bytes 8388608
  81.3 18.3 %copy.75 = bf16[1,32,512,1,128]{2,4,1,3,0:T(8,128)(2,1)} copy(bf16[1,32,512,1,128]{4,3,2,1,0:T(2,128)(2,1)} %get-tuple-element.14) | data formatting | bytes 8388608
  127.0 17.4 %fusion.37 = bf16[32,512,2,128]{1,3,2,0:T(8,128)(2,1)} fusion(bf16[32,512,1,128]{1,3,2,0:T(8,128)(2,1)} %copy-done.4, bf16[32,512,1,128]{1,3,2,0:T(8,128)(2,1)} %copy-done.3, f32[32,128,512,2,1]{2,1,4,3,0:T(8,128)} %fusion.36, f32[512,1,512,2]{2,0,3,1:T(8,128)} %copy-done.8, f32[512,1,512,2]{2,0,3,1:T(8,128)} %copy-done.10), kind=kOutput, calls=%fused_computation.63 | convolution fusion | flops 8620343296 | bytes 37748736 | tf_op jit(solution)/shard_map/kpxr,yxrz->ykpz/dot_general | solution.py:33
  144.4 21.3 %copy.31 = bf16[32,512,2,128]{3,2,0,1:T(2,128)(2,1)} copy(bf16[32,512,2,128]{1,3,2,0:T(8,128)(2,1)} %fusion.37) | data formatting | bytes 16777216 | tf_op jit(solution)/shard_map/convert_element_type | solution.py:89
  173.2 45.1 %copy.38 = f32[1,256,128,2,128]{2,4,3,1,0:T(8,128)} copy(bf16[1,256,128,2,128]{4,3,2,1,0:T(2,128)(2,1)} %param.7) | data formatting | bytes 50331648 | tf_op jit(solution)/shard_map/convert_element_type | solution.py:102
  218.3 105.4 %all-to-all-done = bf16[32,512,2,128]{3,2,0,1:T(2,128)(2,1)} async-done(((bf16[32,512,2,128]{3,2,0,1:T(2,128)(2,1)}), bf16[32,512,2,128]{3,2,0,1:T(2,128)(2,1)}, u32[]{:S(2)}, u32[]{:S(2)}) %all-to-all-start) | async-done | bytes 8388640 | tf_op jit(solution)/shard_map/all_to_all | solution.py:91
  379.9 17.1 %fusion.38 = bf16[512,32,2,128]{0,3,2,1:T(8,128)(2,1)} fusion(bf16[512,32,2,128,1]{0,3,2,4,1:T(8,128)(2,1)} %copy.53, f32[32,128,512,2,1]{2,1,4,3,0:T(8,128)} %fusion.68, f32[512,1,512,2]{2,0,3,1:T(8,128)S(1)} %copy-done.9, f32[512,1,512,2]{2,0,3,1:T(8,128)S(1)} %copy-done.11), kind=kOutput, calls=%fused_computation.64 | convolution fusion | flops 8603566080 | bytes 37748736 | tf_op jit(solution)/shard_map/kpyr,yxrz->kxpz/dot_general | solution.py:40
  436.0 38.3 %fusion.10 = f32[256,128,256]{1,2,0:T(8,128)} fusion(bf16[256,128,128]{2,1,0:T(8,128)(2,1)} %param.8, f32[256,128,256]{1,2,0:T(8,128)} %bitcast.152, bf16[256,128,256]{2,1,0:T(8,128)(2,1)} %gather_fusion, pred[256]{0:T(512)(128)(4,1)S(1)} %get-tuple-element.5), kind=kOutput, calls=%fused_computation.30 | convolution fusion | flops 4320133120 | bytes 92274944 | tf_op jit(solution)/shard_map/bst,bsc->btc/dot_general | solution.py:104
  474.3 33.4 %copy.39 = f32[256,128,256]{2,0,1:T(8,128)} copy(f32[256,128,256]{1,2,0:T(8,128)} %fusion.10) | data formatting | bytes 67108864 | tf_op jit(solution)/shard_map/bst,bsc->btc/dot_general | solution.py:104
  507.7 20.8 %convolution_convert_fusion = bf16[128,128,256]{2,0,1:T(8,128)(2,1)} fusion(f32[256,128,256]{2,0,1:T(8,128)} %copy.39, s32[256]{0:T(256)S(1)} %get-tuple-element.6), kind=kOutput, calls=%fused_computation.60 | convolution fusion | flops 12889128960 | bytes 41944064 | tf_op jit(solution)/shard_map/bl,btc->ltc/dot_general | solution.py:108
  541.1 18.0 %copy.40 = bf16[4,128,32,256]{1,0,3,2:T(4,128)(2,1)} copy(bf16[4,128,32,256]{3,0,2,1:T(4,128)(2,1)} %bitcast.157) | data formatting | bytes 16777216 | tf_op jit(solution)/shard_map/transpose | solution.py:113
  589.1 16.9 %fusion.39 = bf16[512,32,2,128]{0,3,2,1:T(8,128)(2,1)} fusion(bf16[512,32,2,128,1]{0,3,2,1,4:T(8,128)(2,1)} %reshape.239, f32[32,128,512,2,1]{2,1,4,3,0:T(8,128)} %fusion.32, f32[512,1,512,2]{2,0,3,1:T(8,128)S(1)} %copy-done.6, f32[512,1,512,2]{2,0,3,1:T(8,128)S(1)} %copy-done.5), kind=kOutput, calls=%fused_computation.65 | convolution fusion | flops 8603566080 | bytes 37748736 | tf_op jit(solution)/shard_map/kpyr,yxrz->kxpz/dot_general | solution.py:40
  606.1 21.2 %copy.41 = bf16[512,32,2,128]{3,2,1,0:T(2,128)(2,1)} copy(bf16[512,32,2,128]{0,3,2,1:T(8,128)(2,1)} %fusion.39) | data formatting | bytes 16777216 | tf_op jit(solution)/shard_map/convert_element_type | solution.py:116
  627.3 218.8 %all_to_all.36 = bf16[512,32,2,128]{3,2,1,0:T(2,128)(2,1)} all-to-all(bf16[512,32,2,128]{3,2,1,0:T(2,128)(2,1)} %copy.41), channel_id=1, replica_groups=mesh['pen'=16,'coil'=2] {'pen'}, dimensions={0} | all-to-all | bytes 16777216 | tf_op jit(solution)/shard_map/all_to_all | solution.py:118
  878.8 19.0 %fusion.3 = f32[32,512,2,128]{1,3,2,0:T(8,128)} fusion(f32[32,128,512,2,1]{2,1,4,3,0:T(8,128)} %fusion.65, bf16[32,512,2,128,1]{3,1,2,4,0:T(8,128)(2,1)} %bitcast.160, f32[512,1,512,2]{2,0,3,1:T(8,128)} %get-tuple-element.17, f32[512,1,512,2]{2,0,3,1:T(8,128)S(1)} %copy-done.5), kind=kOutput, calls=%fused_computation.12 | convolution fusion | flops 8599371776 | bytes 46137344 | tf_op jit(solution)/shard_map/kpxr,yxrz->ykpz/dot_general | solution.py:33
  922.0 17.4 %copy.46 = f32[32,512,2,128]{3,1,2,0:T(8,128)} copy(f32[32,512,2,128]{1,3,2,0:T(8,128)} %pad_maximum_fusion) | data formatting | bytes 33554432 | tf_op jit(solution)/shard_map/stack | solution.py:122
  956.9 23.7 %fusion.15 = f32[32,257,2,127]{1,3,2,0:T(8,128)} fusion(s32[]{:T(128)S(6)} %select_n.65, s32[]{:T(128)S(6)} %add.170, f32[32,512,2,128]{1,3,2,0:T(8,128)} %copy.28), kind=kLoop, calls=%fused_computation.33 | loop fusion | flops 2088896 | bytes 25132808 | tf_op jit(solution)/shard_map/sub | solution.py:52
  980.7 25.5 %add_reduce_fusion = f32[32,257,128]{1,2,0:T(8,128)} fusion(f32[32,257,2,127]{1,3,2,0:T(8,128)} %fusion.15, f32[257]{0:T(512)S(1)} %get-tuple-element.25, s32[]{:T(128)S(6)} %select_n.65, f32[32,512,2,128]{1,3,2,0:T(8,128)} %copy.28, s32[]{:T(128)S(6)} %add.169, f32[32]{0:T(128)S(1)} %get-tuple-element.26, f32[1,258,2,128]{1,3,2,0:T(8,128)S(1)} %collective-permute-done, ...), kind=kLoop, calls=%fused_computation.40 | loop fusion | flops 22106112 | bytes 38062988 | tf_op jit(solution)/shard_map/reduce_sum | solution.py:55
  1010.7 36.8 %divide_multiply_fusion.2 = (f32[32,257,2,128]{1,3,2,0:T(8,128)}, f32[32,257,2,128]{1,3,2,0:T(8,128)}, f32[32,257,2,128]{1,3,2,0:T(8,128)}) fusion(f32[32,257]{1,0:T(8,128)S(1)} %and_convert_fusion, f32[32,257,128]{1,2,0:T(8,128)S(1)} %add_sqrt_fusion, f32[32]{0:T(128)S(1)} %get-tuple-element.26, s32[]{:T(128)S(6)} %select_n.65, ...), kind=kLoop, calls=%fused_computation.39 | loop fusion | flops 23158784 | bytes 63360012 | tf_op jit(solution)/shard_map/mul | solution.py:60
  1072.1 257.1 %all-gather.3.cloned.1.call-done = f32[64,512,2,128]{3,1,2,0:T(8,128)} async-done(((f32[32,512,2,128]{3,1,2,0:T(8,128)}), f32[64,512,2,128]{3,1,2,0:T(8,128)}) %all-gather.3.cloned.1.call-update) | async-done | bytes 33554448 | tf_op jit(solution)/shard_map/all_gather | solution.py:126
  1329.3 19.1 %reduce_sum.18 = f32[32,512,2,128]{3,1,2,0:T(8,128)} reduce(f32[2,32,512,2,128]{4,2,3,1,0:T(8,128)} %bitcast.154, f32[]{:T(128)} %constant.68.clone.1), dimensions={0}, to_apply=%region_0.1 | reduce | flops 4194304 | bytes 50331652 | tf_op jit(solution)/shard_map/reduce_sum | solution.py:126
  1365.1 28.6 %fusion.30 = f32[32,256,2,128]{1,3,2,0:T(8,128)} fusion(f32[32,256,2,128]{1,3,2,0:T(8,128)} %copy.76, f32[32,257,2,128]{1,3,2,0:T(8,128)} %get-tuple-element.15, f32[32,257,2,128]{1,3,2,0:T(8,128)} %get-tuple-element.12, f32[32,257,2,128]{1,3,2,0:T(8,128)} %get-tuple-element.11, f32[31,257,2,128]{1,3,2,0:T(8,128)} %slice.90, ...), kind=kLoop, calls=%fused_computation.50 | loop fusion | flops 16777216 | bytes 67076096 | tf_op jit(solution)/shard_map/add | solution.py:143
  (69 shorter events, 319.6 us)
Async XLA Ops:
  99.6 10.2 copy-start.1
  99.6 10.2 copy-start.2
  109.7 3.3 copy-start.3
  109.7 4.4 copy-start.4
  112.9 1.9 copy-start.8
  112.9 2.6 copy-start.10
  165.7 158.0 %all-to-all-start = ((bf16[32,512,2,128]{3,2,0,1:T(2,128)(2,1)}), bf16[32,512,2,128]{3,2,0,1:T(2,128)(2,1)}, u32[]{:S(2)}, u32[]{:S(2)}) async-start(bf16[32,512,2,128]{3,2,0,1:T(2,128)(2,1)} %copy.31), calls=%async_computation | async-start | bytes 16777216 | tf_op jit(solution)/shard_map/all_to_all | solution.py:91
  173.1 1156.1 %all-gather.3.cloned.1.call-start = ((), (), s32[]{:S(2)}) async-start(), calls=%async_computation.2 | async-start | bytes 50331648 | tf_op jit(solution)/shard_map/all_gather | solution.py:126
  173.2 45.1 %copy-start.12 = (s32[256]{0:T(256)S(1)}, s32[256]{0:T(256)}, u32[]{:S(2)}) copy-start(s32[256]{0:T(256)} %param.9) | copy-start | bytes 3076
  349.5 14.0 copy-start.9
  363.5 16.4 %copy-start.11 = (f32[512,1,512,2]{2,0,3,1:T(8,128)S(1)}, f32[512,1,512,2]{2,0,3,1:T(8,128)}, u32[]{:S(2)}) copy-start(f32[512,1,512,2]{2,0,3,1:T(8,128)} %copy-done.10) | copy-start | bytes 6291460
  559.1 13.2 copy-start.5
  572.3 16.8 %copy-start.6 = (f32[512,1,512,2]{2,0,3,1:T(8,128)S(1)}, f32[512,1,512,2]{2,0,3,1:T(8,128)}, u32[]{:S(2)}) copy-start(f32[512,1,512,2]{2,0,3,1:T(8,128)} %get-tuple-element.17) | copy-start | bytes 6291460
  855.0 9.1 copy-start.7
  878.8 19.0 %copy-start = (bf16[1,32,512,1,128]{2,4,1,3,0:T(8,128)(2,1)S(1)}, bf16[1,32,512,1,128]{2,4,1,3,0:T(8,128)(2,1)}, u32[]{:S(2)}) copy-start(bf16[1,32,512,1,128]{2,4,1,3,0:T(8,128)(2,1)} %copy.74) | copy-start | bytes 12582916
  940.7 40.0 %collective-permute-start = (f32[1,258,2,128]{1,3,2,0:T(8,128)S(1)}, f32[1,258,2,128]{1,3,2,0:T(8,128)S(1)}, u32[]{:S(2)}, u32[]{:S(2)}) collective-permute-start(f32[1,258,2,128]{1,3,2,0:T(8,128)S(1)} %pad_dynamic-slice_fusion.4), channel_id=1, source_target_pairs={{2,0},{4,2},{6,4},{8,6},{10,8},{12,10},{14,12},{16,14},{18,16},{20... | collective-permute-start | bytes 792584 | tf_op jit(solution)/shard_map/ppermute | solution.py:16
  1068.9 296.2 %collective-permute-start.1 = (f32[1,257,2,128]{1,3,2,0:T(8,128)S(1)}, f32[1,257,2,128]{1,3,2,0:T(8,128)S(1)}, u32[]{:S(2)}, u32[]{:S(2)}) collective-permute-start(f32[1,257,2,128]{1,3,2,0:T(8,128)S(1)} %slice.89), channel_id=1, source_target_pairs={{0,2},{2,4},{4,6},{6,8},{8,10},{10,12},{12,14},{14,16},{16,18},{18... | collective-permute-start | bytes 789512 | tf_op jit(solution)/shard_map/ppermute | solution.py:16
Sparse Core Ops, SparseCore 0:
  939.6 389.6 all-gather.2
